TPU v7x, 32 devices: a whole 2x2x4 slice. The times are simulated.
32 devices in a mesh: fsdp: 4 (over y, x), heads: 2 (over core), tensor: 4 (over z).
Axes of the slice: x: 2, y: 2, z: 4, core: 2. Of those that a mesh axis runs over, the one named last changes fastest.
Arguments:
- inputs: float32 [32, 729, 1152], P(('fsdp', 'heads', 'tensor')), may hold values from -6 to 6
- cotangent: float32 [32, 729, 1152], P(('fsdp', 'heads', 'tensor')), may hold values from -6 to 6
- image_adapter_index: int32 [32], replicated, may hold values from 0 to 7
- first_norm_gain: float32 [1152], replicated, may hold values from 0.5 to 1.5
- first_norm_bias: float32 [1152], replicated, may hold values from -3 to 3
- second_norm_gain: float32 [1152], replicated, may hold values from 0.5 to 1.5
- second_norm_bias: float32 [1152], replicated, may hold values from -3 to 3
- query_key_value_weight: bfloat16 [1152, 3, 1152], P('fsdp', None, 'heads'), may hold values from -0.1875 to 0.1875
- attention_output_weight: bfloat16 [1152, 1152], P('fsdp', 'heads'), may hold values from -3 to 3
- up_weight: bfloat16 [1152, 4304], P('fsdp', 'tensor'), may hold values from -0.1875 to 0.1875
- down_weight: bfloat16 [1152, 4304], P('fsdp', 'tensor'), may hold values from -0.09375 to 0.09375
- up_projection_bias: bfloat16 [4304], P('tensor'), may hold values from -3 to 3
- down_projection_bias: bfloat16 [1152], replicated, may hold values from -3 to 3
- query_key_value_adapter_first: bfloat16 [3, 8, 1152, 16], replicated, may hold values from -0.1875 to 0.1875
- query_key_value_adapter_second: bfloat16 [3, 8, 16, 1152], P(None, None, None, 'heads'), may hold values from -0.75 to 0.75
- projection_adapter_first: bfloat16 [8, 1152, 16], P(None, 'heads'), may hold values from -3 to 3
- projection_adapter_second: bfloat16 [8, 16, 1152], replicated, may hold values from -0.75 to 0.75
- up_adapter_first: bfloat16 [8, 1152, 16], replicated, may hold values from -0.1875 to 0.1875
- up_adapter_second: bfloat16 [8, 16, 4304], P(None, None, 'tensor'), may hold values from -0.75 to 0.75
- down_adapter_first: bfloat16 [8, 16, 4304], P(None, None, 'tensor'), may hold values from -0.09375 to 0.09375
- down_adapter_second: bfloat16 [8, 16, 1152], replicated, may hold values from -0.75 to 0.75
Outputs:
- layer_output: float32 [32, 729, 1152], P(('fsdp', 'heads', 'tensor'))
- grad_input: float32 [32, 729, 1152], P(('fsdp', 'heads', 'tensor'))
- grad_qkv_in: float32 [3, 8, 1152, 16], replicated
- grad_qkv_out: float32 [3, 8, 16, 1152], P(None, None, None, 'heads')
- grad_proj_in: float32 [8, 1152, 16], P(None, 'heads')
- grad_proj_out: float32 [8, 16, 1152], replicated
- grad_up_in: float32 [8, 1152, 16], replicated
- grad_up_out: float32 [8, 16, 4304], P(None, None, 'tensor')
- grad_down_in: float32 [8, 16, 4304], P(None, None, 'tensor')
- grad_down_out: float32 [8, 16, 1152], replicated
All inputs are finite; a program needn't handle non-finite values.
Results may differ from a plain program's by a relative error of at most 0.02.
Values may be sent and summed in bfloat16 or wider, within the bound.
A program may use at most 256 MiB of HBM per device.

v0:
```python
import jax
import jax.numpy as jnp
from jax import lax
from jax.sharding import PartitionSpec as P

HEAD_DIM = 72
highest_precision = lax.Precision.HIGHEST
norm_eps = 1e-06


def normalize(values, gain, bias):
    mean = jnp.mean(values, axis=-1, keepdims=True)
    centred = values - mean
    inverse = lax.rsqrt(jnp.mean(centred * centred, axis=-1, keepdims=True) + norm_eps)
    unit = centred * inverse
    return (unit * gain + bias, unit, inverse)


def normalize_back(grad_norm, unit, inverse, gain):
    scaled = grad_norm * gain
    return inverse * (
        scaled
        - jnp.mean(scaled, axis=-1, keepdims=True)
        - unit * jnp.mean(scaled * unit, axis=-1, keepdims=True)
    )


def gelu_tanh(values):
    return jax.nn.gelu(values, approximate=True)


def one_hot(ids, count):
    return (ids[:, None] == jnp.arange(count, dtype=jnp.int32)[None, :]).astype(jnp.float32)


def by_adapter(hot, per_image):
    return jnp.einsum("ia,ixy->axy", hot, per_image, precision=highest_precision)


def attend_forward(operands):
    query, keyed, valued = operands
    scores = jnp.einsum(
        "qhd,khd->hqk", query, keyed, preferred_element_type=jnp.float32
    ) * HEAD_DIM ** (-0.5)
    top = jnp.max(scores, axis=-1, keepdims=True)
    weights = jnp.exp(scores - top)
    total = jnp.sum(weights, axis=-1, keepdims=True)
    probs = (weights / total).astype(jnp.bfloat16)
    mixed_heads = jnp.einsum("hqk,khd->qhd", probs, valued, preferred_element_type=jnp.float32)
    return (mixed_heads.astype(jnp.bfloat16), (top + jnp.log(total))[..., 0])


def attend_back(operands):
    query, keyed, valued, grad_mixed, log_total = operands
    scale = HEAD_DIM ** (-0.5)
    scores = jnp.einsum("qhd,khd->hqk", query, keyed, preferred_element_type=jnp.float32) * scale
    probs = jnp.exp(scores - log_total[..., None])
    grad_probs = jnp.einsum("qhd,khd->hqk", grad_mixed, valued, preferred_element_type=jnp.float32)
    grad_values = jnp.einsum(
        "hqk,qhd->khd", probs.astype(jnp.bfloat16), grad_mixed, preferred_element_type=jnp.float32
    )
    inner = jnp.sum(probs * grad_probs, axis=-1, keepdims=True)
    grad_scores = (probs * (grad_probs - inner)).astype(jnp.bfloat16)
    grad_query = (
        jnp.einsum("hqk,khd->qhd", grad_scores, keyed, preferred_element_type=jnp.float32) * scale
    )
    grad_keys = (
        jnp.einsum("hqk,qhd->khd", grad_scores, query, preferred_element_type=jnp.float32) * scale
    )
    return (grad_query, grad_keys, grad_values)


def per_device(
    inputs,
    cotangent,
    image_adapter_index,
    first_norm_gain,
    first_norm_bias,
    second_norm_gain,
    second_norm_bias,
    query_key_value_weight,
    attention_output_weight,
    up_weight,
    down_weight,
    up_projection_bias,
    down_projection_bias,
    query_key_value_adapter_first,
    query_key_value_adapter_second,
    projection_adapter_first,
    projection_adapter_second,
    up_adapter_first,
    up_adapter_second,
    down_adapter_first,
    down_adapter_second,
):
    head_count = lax.axis_size("heads")
    unit_count = lax.axis_size("tensor")
    fsdp_index = lax.axis_index("fsdp")
    head_index = lax.axis_index("heads")
    unit_index = lax.axis_index("tensor")
    images, length, width = inputs.shape
    adapter_factors = query_key_value_adapter_first.shape[1]
    local = jnp.arange(images, dtype=jnp.int32)
    group = fsdp_index * head_count
    own_rows = ((group + head_index) * unit_count + unit_index) * images + local
    head_rows = (
        ((group + jnp.arange(head_count, dtype=jnp.int32))[:, None] * unit_count + unit_index)
        * images
        + local[None, :]
    ).reshape(-1)
    unit_rows = (
        ((group + head_index) * unit_count + jnp.arange(unit_count, dtype=jnp.int32))[:, None]
        * images
        + local[None, :]
    ).reshape(-1)
    owned_numbers = image_adapter_index[own_rows]
    head_numbers = image_adapter_index[head_rows]
    unit_numbers = image_adapter_index[unit_rows]
    query_key_value_whole, output_whole_weight, up_rows, down_rows = (
        lax.all_gather(query_key_value_weight, "fsdp", axis=0, tiled=True),
        lax.all_gather(attention_output_weight, "fsdp", axis=0, tiled=True),
        lax.all_gather(up_weight, "fsdp", axis=0, tiled=True),
        lax.all_gather(down_weight, "fsdp", axis=0, tiled=True),
    )
    norm1, unit1, inverse1 = normalize(inputs, first_norm_gain, first_norm_bias)
    ln1_all = lax.all_gather(norm1.astype(jnp.bfloat16), "heads", axis=0, tiled=True)
    (
        query_key_value_attention,
        output_attention_part,
        query_key_value_output_weight,
        projection_input_weight,
    ) = (
        query_key_value_whole,
        output_whole_weight,
        query_key_value_adapter_second,
        projection_adapter_first,
    )
    seen = ln1_all.shape[0]
    query_key_value_input_selected = query_key_value_adapter_first[:, head_numbers]
    qkv_out_sel = query_key_value_output_weight[:, head_numbers]
    query_key_value_middle = jnp.einsum(
        "obl,holm->hobm",
        ln1_all,
        query_key_value_input_selected,
        preferred_element_type=jnp.float32,
    )
    projected = jnp.einsum(
        "isd,djf->jisf", ln1_all, query_key_value_attention, preferred_element_type=jnp.float32
    )
    projected = projected + jnp.einsum(
        "klty,klye->klte",
        query_key_value_middle,
        qkv_out_sel.astype(jnp.float32),
        precision=highest_precision,
    )
    proj_low = projected.astype(jnp.bfloat16)
    local_width = proj_low.shape[-1]
    heads_local = local_width // HEAD_DIM
    shaped = proj_low.reshape(3, seen, length, heads_local, HEAD_DIM)
    mixed_heads, log_total = lax.map(attend_forward, (shaped[0], shaped[1], shaped[2]))
    mixed_heads = mixed_heads.reshape(seen, length, local_width)
    proj_in_sel = projection_input_weight[head_numbers]
    projection_output_selected = projection_adapter_second[head_numbers]
    projection_adapter_middle = jnp.einsum(
        "lby,lyg->lbg", mixed_heads, proj_in_sel, preferred_element_type=jnp.float32
    )
    attention_branch = jnp.einsum(
        "ise,de->isd", mixed_heads, output_attention_part, preferred_element_type=jnp.float32
    )
    attention_branch = attention_branch + jnp.einsum(
        "cmt,ctf->cmf",
        projection_adapter_middle,
        projection_output_selected.astype(jnp.float32),
        precision=highest_precision,
    )
    hidden = inputs + lax.psum_scatter(
        attention_branch.astype(jnp.bfloat16), "heads", scatter_dimension=0, tiled=True
    ).astype(jnp.float32)
    norm2, unit2, inverse2 = normalize(hidden, second_norm_gain, second_norm_bias)
    second_norm_reduced = norm2.astype(jnp.bfloat16)
    up_adapter_middle = jnp.einsum(
        "ego,eoh->egh",
        second_norm_reduced,
        up_adapter_first[owned_numbers],
        preferred_element_type=jnp.float32,
    ).astype(jnp.bfloat16)
    ln2_in, up_mid_in = (
        lax.all_gather(second_norm_reduced, "tensor", axis=0, tiled=True),
        lax.all_gather(up_adapter_middle, "tensor", axis=0, tiled=True),
    )
    up_cols, down_cols, bias_cols = (up_rows, down_rows, up_projection_bias)
    up_output_columns, down_input_columns = (up_adapter_second, down_adapter_first)
    up_input_selected = up_adapter_first[unit_numbers]
    up_out_sel = up_output_columns[unit_numbers]
    down_in_sel = down_input_columns[unit_numbers]
    down_output_selected = down_adapter_second[unit_numbers]
    residual_before = jnp.einsum(
        "isd,df->isf", ln2_in, up_cols, preferred_element_type=jnp.float32
    ) + bias_cols.astype(jnp.float32)
    residual_before = residual_before + jnp.einsum(
        "cbd,cdp->cbp",
        up_mid_in.astype(jnp.float32),
        up_out_sel.astype(jnp.float32),
        precision=highest_precision,
    )
    act_low = gelu_tanh(residual_before).astype(jnp.bfloat16)
    down_adapter_middle = jnp.einsum(
        "pco,pqo->pcq", act_low, down_in_sel, preferred_element_type=jnp.float32
    )
    mlp_part = jnp.einsum("isf,df->isd", act_low, down_cols, preferred_element_type=jnp.float32)
    mlp_part = mlp_part + jnp.einsum(
        "cmt,ctf->cmf",
        down_adapter_middle,
        down_output_selected.astype(jnp.float32),
        precision=highest_precision,
    )
    mlp_sum = lax.psum_scatter(
        mlp_part.astype(jnp.bfloat16), "tensor", scatter_dimension=0, tiled=True
    ).astype(jnp.float32)
    layer_output = hidden + mlp_sum + down_projection_bias.astype(jnp.float32)
    grad_mlp = cotangent.astype(jnp.bfloat16)
    grad_mlp_in = lax.all_gather(grad_mlp, "tensor", axis=0, tiled=True)
    grad_down_mid = jnp.einsum(
        "isd,ird->isr", grad_mlp_in, down_output_selected, preferred_element_type=jnp.float32
    )
    grad_act = jnp.einsum("isd,df->isf", grad_mlp_in, down_cols, preferred_element_type=jnp.float32)
    grad_act = grad_act + jnp.einsum(
        "cbd,cdp->cbp", grad_down_mid, down_in_sel.astype(jnp.float32), precision=highest_precision
    )
    ignored, gelu_pull = jax.vjp(gelu_tanh, residual_before)
    grad_before = gelu_pull(grad_act)[0].astype(jnp.bfloat16)
    grad_up_mid = jnp.einsum(
        "pco,pqo->pcq", grad_before, up_out_sel, preferred_element_type=jnp.float32
    )
    grad_ln2 = jnp.einsum("isf,df->isd", grad_before, up_cols, preferred_element_type=jnp.float32)
    grad_ln2 = grad_ln2 + jnp.einsum(
        "isr,idr->isd",
        grad_up_mid,
        up_input_selected.astype(jnp.float32),
        precision=highest_precision,
    )
    grad_ln2 = lax.psum_scatter(
        grad_ln2.astype(jnp.bfloat16), "tensor", scatter_dimension=0, tiled=True
    ).astype(jnp.float32)
    grad_hidden = cotangent + normalize_back(grad_ln2, unit2, inverse2, second_norm_gain)
    mlp_hot = one_hot(unit_numbers, adapter_factors)
    grad_up_in_part = by_adapter(
        mlp_hot, jnp.einsum("isd,isr->idr", ln2_in, grad_up_mid, precision=highest_precision)
    )
    grad_up_out_part = by_adapter(
        mlp_hot,
        jnp.einsum("isr,isf->irf", up_mid_in, grad_before, preferred_element_type=jnp.float32),
    )
    grad_down_in_part = by_adapter(
        mlp_hot, jnp.einsum("isr,isf->irf", grad_down_mid, act_low, precision=highest_precision)
    )
    grad_down_out_part = by_adapter(
        mlp_hot,
        jnp.einsum("isr,isd->ird", down_adapter_middle, grad_mlp_in, precision=highest_precision),
    )
    grad_branch = lax.all_gather(grad_hidden.astype(jnp.bfloat16), "heads", axis=0, tiled=True)
    grad_proj_mid = jnp.einsum(
        "isd,ird->isr", grad_branch, projection_output_selected, preferred_element_type=jnp.float32
    )
    grad_mixed = jnp.einsum(
        "isd,de->ise", grad_branch, output_attention_part, preferred_element_type=jnp.float32
    )
    grad_mixed = grad_mixed + jnp.einsum(
        "isr,ier->ise", grad_proj_mid, proj_in_sel.astype(jnp.float32), precision=highest_precision
    )
    grad_mixed = grad_mixed.astype(jnp.bfloat16).reshape(seen, length, heads_local, HEAD_DIM)
    grad_query, grad_keys, grad_values = lax.map(
        attend_back, (shaped[0], shaped[1], shaped[2], grad_mixed, log_total)
    )
    grad_proj = (
        jnp.stack([grad_query, grad_keys, grad_values])
        .reshape(3, seen, length, local_width)
        .astype(jnp.bfloat16)
    )
    grad_qkv_mid = jnp.einsum(
        "jisf,jirf->jisr", grad_proj, qkv_out_sel, preferred_element_type=jnp.float32
    )
    grad_ln1 = jnp.einsum(
        "jisf,djf->isd", grad_proj, query_key_value_attention, preferred_element_type=jnp.float32
    )
    grad_ln1 = grad_ln1 + jnp.einsum(
        "jisr,jidr->isd",
        grad_qkv_mid,
        query_key_value_input_selected.astype(jnp.float32),
        precision=highest_precision,
    )
    grad_ln1 = lax.psum_scatter(
        grad_ln1.astype(jnp.bfloat16), "heads", scatter_dimension=0, tiled=True
    ).astype(jnp.float32)
    grad_input = grad_hidden + normalize_back(grad_ln1, unit1, inverse1, first_norm_gain)
    attn_hot = one_hot(head_numbers, adapter_factors)
    qkv_in_image = jnp.einsum("isd,jisr->jidr", ln1_all, grad_qkv_mid, precision=highest_precision)
    grad_qkv_in_part = jnp.einsum(
        "ia,jidr->jadr", attn_hot, qkv_in_image, precision=highest_precision
    )
    qkv_out_image = jnp.einsum(
        "jisr,jisf->jirf", query_key_value_middle, grad_proj, precision=highest_precision
    )
    grad_qkv_out_part = jnp.einsum(
        "ia,jirf->jarf", attn_hot, qkv_out_image, precision=highest_precision
    )
    grad_proj_in_part = by_adapter(
        attn_hot,
        jnp.einsum("ise,isr->ier", mixed_heads, grad_proj_mid, precision=highest_precision),
    )
    grad_proj_out_part = by_adapter(
        attn_hot,
        jnp.einsum(
            "isr,isd->ird", projection_adapter_middle, grad_branch, precision=highest_precision
        ),
    )
    grad_qkv_in, grad_proj_out, grad_up_in, grad_down_out = lax.psum(
        (grad_qkv_in_part, grad_proj_out_part, grad_up_in_part, grad_down_out_part),
        ("fsdp", "heads", "tensor"),
    )
    grad_qkv_out, grad_proj_in = lax.psum(
        (grad_qkv_out_part, grad_proj_in_part), ("fsdp", "tensor")
    )
    grad_up_out, grad_down_in = (
        lax.psum(grad_up_out_part.astype(jnp.bfloat16), ("fsdp", "heads")).astype(jnp.float32),
        lax.psum(grad_down_in_part.astype(jnp.bfloat16), ("fsdp", "heads")).astype(jnp.float32),
    )
    return (
        layer_output,
        grad_input,
        grad_qkv_in,
        grad_qkv_out,
        grad_proj_in,
        grad_proj_out,
        grad_up_in,
        grad_up_out,
        grad_down_in,
        grad_down_out,
    )


def solution(mesh):
    in_specs = (
        P(("fsdp", "heads", "tensor"), None, None),
        P(("fsdp", "heads", "tensor"), None, None),
        P(),
        P(),
        P(),
        P(),
        P(),
        P("fsdp", None, "heads"),
        P("fsdp", "heads"),
        P("fsdp", "tensor"),
        P("fsdp", "tensor"),
        P("tensor"),
        P(),
        P(),
        P(None, None, None, "heads"),
        P(None, "heads", None),
        P(),
        P(),
        P(None, None, "tensor"),
        P(None, None, "tensor"),
        P(),
    )
    out_specs = (
        P(("fsdp", "heads", "tensor"), None, None),
        P(("fsdp", "heads", "tensor"), None, None),
        P(),
        P(None, None, None, "heads"),
        P(None, "heads", None),
        P(),
        P(),
        P(None, None, "tensor"),
        P(None, None, "tensor"),
        P(),
    )
    return jax.shard_map(
        per_device, mesh=mesh, in_specs=in_specs, out_specs=out_specs, check_vma=False
    )
```

profile of v0, /device:TPU:0, one launch (start us, length us, event | category | flops | bytes accessed | tf_op | source)
XLA Modules:
  0.0 1267.5 jit_solution(7760785568148674721)
XLA Ops:
  25.9 7.4 all-gather.11.cloned.1.call-done
  36.3 54.6 %all-gather.13.cloned.1.call-done = bf16[1152,3,576]{2,0,1:T(8,128)(2,1)} async-done(((bf16[288,3,576]{2,0,1:T(8,128)(2,1)}), bf16[1152,3,576]{2,0,1:T(8,128)(2,1)}) %all-gather.13.cloned.1.call-update) | async-done | bytes 3981328 | tf_op jit(solution)/shard_map/all_gather | solution.py:120
  90.9 10.7 fusion.59
  101.6 5.3 fusion.51
  109.1 57.2 %while.28 = (s32[]{:T(128)}, bf16[2,729,8,72]{1,3,2,0:T(8,128)(2,1)}, f32[2,8,729]{2,1,0:T(8,128)S(1)}, bf16[2,729,8,72]{1,3,2,0:T(8,128)(2,1)}, bf16[2,729,8,72...) while((s32[]{:T(128)}, bf16[2,729,8,72]{1,3,2,0:T(8,128)(2,1)}, ...), condition=%wide.region_5.6_spmd, body=%wide.region_2.5_spmd.sunk | while | flops 1263117824 | bytes 55831608 | solution.py:160
  109.1 9.9 multiply_reduce_fusion.8
  119.0 9.2 fusion.206
  128.2 9.3 fusion.207
  137.5 9.9 multiply_reduce_fusion.8
  147.4 9.2 fusion.206
  156.6 9.3 fusion.207
  168.9 5.0 fusion.84
  183.0 6.8 reduce-scatter.5.cloned.1.call-done
  202.4 102.8 %all-gather.23.cloned.1.call-done = bf16[4,729,1152]{2,1,0:T(8,128)(2,1)} async-done(((bf16[1,729,1152]{2,1,0:T(8,128)(2,1)}), bf16[4,729,1152]{2,1,0:T(8,128)(2,1)}) %all-gather.23.cloned.1.call-update) | async-done | bytes 6718480 | tf_op jit(solution)/shard_map/all_gather | solution.py:222
  310.0 34.9 %all-gather.21.cloned.1.call-done = bf16[1152,1076]{1,0:T(8,128)(2,1)} async-done(((bf16[288,1076]{1,0:T(8,128)(2,1)}), bf16[1152,1076]{1,0:T(8,128)(2,1)}) %all-gather.21.cloned.1.call-update) | async-done | bytes 2479120 | tf_op jit(solution)/shard_map/all_gather | solution.py:123
  344.9 14.5 %fusion.69 = f32[4,729,1076]{1,2,0:T(8,128)} fusion(bf16[4,729,1152]{2,1,0:T(8,128)(2,1)} %all-gather.23.cloned.1.call-done, bf16[1152,1076]{1,0:T(8,128)(2,1)} %all-gather.21.cloned.1.call-done), kind=kOutput, calls=%fused_computation.114 | convolution fusion | flops 7229067264 | bytes 21748032 | tf_op jit(solution)/shard_map/isd,df->isf/dot_general | solution.py:226
  359.9 13.3 %all-gather.1 = bf16[4,729,16]{1,2,0:T(8,128)(2,1)S(1)} all-gather(bf16[1,729,16]{1,2,0:T(8,128)(2,1)S(1)} %fusion.92), channel_id=2, replica_groups=mesh['fsdp'=4,'heads'=2,'tensor'=4] {'tensor'}, dimensions={0}, use_global_device_ids=true | all-gather | bytes 116640 | tf_op jit(solution)/shard_map/all_gather | solution.py:189
  373.2 13.1 %all-gather.19.cloned.1.call-done = bf16[1152,1076]{1,0:T(8,128)(2,1)} async-done(((bf16[288,1076]{1,0:T(8,128)(2,1)}), bf16[1152,1076]{1,0:T(8,128)(2,1)}) %all-gather.19.cloned.1.call-update) | async-done | bytes 2479120 | tf_op jit(solution)/shard_map/all_gather | solution.py:122
  386.4 124.8 %all-gather.17.cloned.1.call-done = bf16[4,729,1152]{2,1,0:T(8,128)(2,1)} async-done(((bf16[1,729,1152]{2,1,0:T(8,128)(2,1)}), bf16[4,729,1152]{2,1,0:T(8,128)(2,1)}) %all-gather.17.cloned.1.call-update) | async-done | bytes 6718480 | tf_op jit(solution)/shard_map/all_gather | solution.py:188
  511.2 12.4 fusion.75
  523.6 10.1 multiply_convert_fusion.1
  533.7 18.5 %fusion.50 = bf16[4,729,1076]{1,2,0:T(8,128)(2,1)S(1)} fusion(f32[4,729,1076]{1,2,0:T(8,128)} %get-tuple-element.204, f32[4,729,1076]{1,2,0:T(8,128)} %fusion.69, f32[4,16,729]{2,1,0:T(8,128)S(1)} %fusion.138, bf16[4,16,1076]{2,1,0:T(8,128)(2,1)S(1)} %gather_fusion.7), kind=kOutput, calls=%fused_computation.72 | convolution fusion | flops 668312192 | bytes 31700512 | tf_op jit(solution)/shard_map/cbd,cdp->cbp/dot_general | solution.py:227
  555.9 13.1 %fusion.73 = f32[4,729,1152]{2,1,0:T(8,128)} fusion(bf16[4,729,1076]{1,2,0:T(8,128)(2,1)S(1)} %fusion.50, bf16[1152,1076]{1,0:T(8,128)(2,1)S(1)} %copy-done.56), kind=kOutput, calls=%fused_computation.118 | convolution fusion | flops 7229067264 | bytes 22191264 | tf_op jit(solution)/shard_map/isf,df->isd/dot_general | solution.py:235
  569.0 10.8 add_convert_fusion
  583.9 13.5 %fusion.71 = f32[4,729,1152]{2,1,0:T(8,128)S(1)} fusion(bf16[4,729,1076]{1,2,0:T(8,128)(2,1)} %get-tuple-element.203, bf16[1152,1076]{1,0:T(8,128)(2,1)S(1)} %copy-done.55), kind=kOutput, calls=%fused_computation.116 | convolution fusion | flops 7229067264 | bytes 22191264 | tf_op jit(solution)/shard_map/isf,df->isd/dot_general | solution.py:210
  597.4 8.5 add_convert_fusion.1
  606.6 90.2 %reduce-scatter.9.cloned.1.call-done = bf16[1,729,1152]{2,1,0:T(8,128)(2,1)} async-done(((bf16[4,729,1152]{2,1,0:T(8,128)(2,1)}), bf16[1,729,1152]{2,1,0:T(8,128)(2,1)}) %reduce-scatter.9.cloned.1.call-update) | async-done | bytes 1679632 | tf_op jit(solution)/shard_map/reduce_scatter | solution.py:242
  700.4 118.0 %reduce-scatter.7.cloned.1.call-done = bf16[1,729,1152]{2,1,0:T(8,128)(2,1)} async-done(((bf16[4,729,1152]{2,1,0:T(8,128)(2,1)}), bf16[1,729,1152]{2,1,0:T(8,128)(2,1)}) %reduce-scatter.7.cloned.1.call-update) | async-done | bytes 1679632 | tf_op jit(solution)/shard_map/reduce_scatter | solution.py:217
  818.4 6.4 fusion.133
  824.9 7.5 fusion.145
  833.7 5.5 fusion.144
  840.5 5.1 fusion.146
  863.4 99.9 %while.29 = (s32[]{:T(128)}, bf16[2,729,8,72]{1,3,2,0:T(8,128)(2,1)}, bf16[2,729,8,72]{1,3,2,0:T(8,128)(2,1)}, bf16[2,729,8,72]{1,3,2,0:T(8,128)(2,1)}, bf16[2,7...) while((s32[]{:T(128)}, ...), condition=%wide.region_15.16_spmd, body=%wide.region_13.15_spmd.sunk | while | flops 3112952320 | bytes 200497152 | solution.py:272
  863.9 10.1 fusion.216
  873.9 8.1 bitcast_dynamic-update-slice_fusion.11
  882.1 12.7 %multiply_reduce_fusion.9 = (f32[8,729]{1,0:T(8,128)S(1)}, f32[8,729,729]{1,2,0:T(8,128)}) fusion(f32[8,729,729]{1,2,0:T(8,128)} %fusion.216, f32[8,729]{1,0:T(8,128)S(1)} %dynamic-slice_bitcast_fusion.2, bf16[2,729,8,72]{1,3,2,0:T(8,128)(2,1)S(1)} %copy-done.13, s32[]{:T(128)S(6)} %copy.187, bf16[2,729,8,72]{1,3,2,0:T(8,128)(2,1)S(1)} %copy-done.9), kind=kOutput, calls=%fused_computation.30.clone.1 | convolution fusion | flops 629220288 | bytes 35830624 | tf_op jit(solution)/shard_map/while/body/eval_jaxpr/qhd,khd->hqk/dot_general | solution.py:58
  894.8 13.2 %multiply_convert_fusion.3 = bf16[8,729,729]{1,2,0:T(8,128)(2,1)S(1)} fusion(f32[8,729,729]{1,2,0:T(8,128)} %get-tuple-element.305, f32[8,729,729]{1,2,0:T(8,128)} %fusion.216, f32[8,729]{1,0:T(8,128)S(1)} %get-tuple-element.306, f32[8,729]{1,0:T(8,128)S(1)} %dynamic-slice_bitcast_fusion.2), kind=kLoop, calls=%fused_computation.29.clone.1 | loop fusion | flops 21257640 | bytes 42561936 | tf_op jit(solution)/shard_map/while/body/eval_jaxpr/convert_element_type | solution.py:63
  913.8 10.0 fusion.216
  923.8 8.1 bitcast_dynamic-update-slice_fusion.11
  932.0 12.6 multiply_reduce_fusion.9
  944.5 13.1 %multiply_convert_fusion.3 = bf16[8,729,729]{1,2,0:T(8,128)(2,1)S(1)} fusion(f32[8,729,729]{1,2,0:T(8,128)} %get-tuple-element.305, f32[8,729,729]{1,2,0:T(8,128)} %fusion.216, f32[8,729]{1,0:T(8,128)S(1)} %get-tuple-element.306, f32[8,729]{1,0:T(8,128)S(1)} %dynamic-slice_bitcast_fusion.2), kind=kLoop, calls=%fused_computation.29.clone.1 | loop fusion | flops 21257640 | bytes 42561936 | tf_op jit(solution)/shard_map/while/body/eval_jaxpr/convert_element_type | solution.py:63
  963.4 6.3 fusion.53
  983.7 11.9 fusion.57
  1004.1 7.2 copy.104
  1011.3 76.5 %all-reduce.9.cloned.1.call-done = (f32[3,8,16,576]{3,1,2,0:T(8,128)}, f32[8,576,16]{1,0,2:T(8,128)}) async-done(((f32[3,8,16,576]{3,1,2,0:T(8,128)}, f32[8,576,16]{1,0,2:T(8,128)}), (f32[3,8,16,576]{3,1,2,0:T(8,128)}, f32[8,576,16]{1,0,2:T(8,128)})) %all-reduce.9.cloned.1.call-update) | async-done | bytes 1179664 | tf_op jit(solution)/shard_map/psum | solution.py:321
  1091.8 142.8 %all-reduce.7.cloned.1.call-done = (f32[3,8,1152,16]{2,1,3,0:T(8,128)}, f32[8,16,1152]{2,0,1:T(8,128)}, f32[8,1152,16]{1,0,2:T(8,128)}, f32[8,16,1152]{2,0,1:T(8,128)}) async-done(((f32[3,8,1152,16]{2,1,3,0:T(8,128)}, f32[8,16,1152]{2,0,1:T(8,128)}, f32[8,1152,16]{1,0,2:T(8,128)}, f32[8,16,1152]{2,0,1:T(8,128)}), (f32[3,8,1152,16]{2,1,3,0:T(8,128)}, f32[8,16,1152]{2,0,1:T(8,128)}, f32[8,1152,16]{1,0,2:T(8,128)}, ...) | async-done | bytes 3538960 | tf_op jit(solution)/shard_map/psum | solution.py:317
  1240.5 6.8 reduce-scatter.11.cloned.1.call-done
  1254.9 5.2 copy.105
  (272 shorter events, 134.1 us)
Async XLA Ops:
  8.0 17.2 %copy-start = (bf16[3,8,1152,16]{2,3,1,0:T(8,128)(2,1)S(1)}, bf16[3,8,1152,16]{2,3,1,0:T(8,128)(2,1)}, u32[]{:S(2)}) copy-start(bf16[3,8,1152,16]{2,3,1,0:T(8,128)(2,1)} %param.38) | copy-start | bytes 2654212
  8.0 8.0 copy-start.42
  8.0 8.0 copy-start.51
  8.0 25.2 %all-gather.11.cloned.1.call-start = ((), (), s32[]{:S(2)}) async-start(), calls=%async_computation.4 | async-start | bytes 5087232 | tf_op jit(solution)/shard_map/all_gather | solution.py:126
  17.9 73.0 %all-gather.13.cloned.1.call-start = ((), (), s32[]{:S(2)}) async-start(), calls=%async_computation.5 | async-start | bytes 5529600 | tf_op jit(solution)/shard_map/all_gather | solution.py:120
  18.6 150.3 %all-gather.15.cloned.1.call-start = ((), (), s32[]{:S(2)}) async-start(), calls=%async_computation.6 | async-start | bytes 1843200 | tf_op jit(solution)/shard_map/all_gather | solution.py:121
  19.4 170.4 %reduce-scatter.5.cloned.1.call-start = ((), (), s32[]{:S(2)}) async-start(), calls=%async_computation.7 | async-start | bytes 5087232 | tf_op jit(solution)/shard_map/reduce_scatter | solution.py:176
  25.2 76.4 %copy-start.32 = (bf16[2,3,16,576]{3,2,1,0:T(8,128)(2,1)}, bf16[2,3,16,576]{3,2,1,0:T(8,128)(2,1)S(1)}, u32[]{:S(2)}) copy-start(bf16[2,3,16,576]{3,2,1,0:T(8,128)(2,1)S(1)} %gather_fusion.2) | copy-start | bytes 331780
  25.8 75.8 %copy-start.11 = (bf16[2,3,1152,16]{2,3,1,0:T(8,128)(2,1)}, bf16[2,3,1152,16]{2,3,1,0:T(8,128)(2,1)S(1)}, u32[]{:S(2)}) copy-start(bf16[2,3,1152,16]{2,3,1,0:T(8,128)(2,1)S(1)} %gather_fusion.1) | copy-start | bytes 663556
  36.3 65.4 %copy-start.25 = (f32[3,2,729,16]{2,3,0,1:T(8,128)}, f32[3,2,729,16]{2,3,0,1:T(8,128)S(1)}, u32[]{:S(2)}) copy-start(f32[3,2,729,16]{2,3,0,1:T(8,128)S(1)} %fusion.86) | copy-start | bytes 839812
  109.1 57.2 %copy-start.21 = (bf16[2,576,16]{1,2,0:T(8,128)(2,1)S(1)}, bf16[2,576,16]{1,2,0:T(8,128)(2,1)}, u32[]{:S(2)}) copy-start(bf16[2,576,16]{1,2,0:T(8,128)(2,1)} %gather_fusion.3) | copy-start | bytes 110596
  166.3 7.6 copy-start.4
  166.3 7.6 copy-start.37
  178.4 126.8 %all-gather.23.cloned.1.call-start = ((), (), s32[]{:S(2)}) async-start(), calls=%async_computation.12 | async-start | bytes 8478720 | tf_op jit(solution)/shard_map/all_gather | solution.py:222
  181.8 163.1 %all-gather.21.cloned.1.call-start = ((), (), s32[]{:S(2)}) async-start(), calls=%async_computation.10 | async-start | bytes 3317760 | tf_op jit(solution)/shard_map/all_gather | solution.py:123
  182.4 204.0 %all-gather.19.cloned.1.call-start = ((), (), s32[]{:S(2)}) async-start(), calls=%async_computation.9 | async-start | bytes 3317760 | tf_op jit(solution)/shard_map/all_gather | solution.py:122
  182.9 328.3 %all-gather.17.cloned.1.call-start = ((), (), s32[]{:S(2)}) async-start(), calls=%async_computation.8 | async-start | bytes 8478720 | tf_op jit(solution)/shard_map/all_gather | solution.py:188
  196.7 500.0 %reduce-scatter.9.cloned.1.call-start = ((), (), s32[]{:S(2)}) async-start(), calls=%async_computation.13 | async-start | bytes 8478720 | tf_op jit(solution)/shard_map/reduce_scatter | solution.py:242
  310.0 49.4 %copy-start.14 = (bf16[1,729,1152]{2,1,0:T(8,128)(2,1)S(1)}, bf16[1,729,1152]{2,1,0:T(8,128)(2,1)}, u32[]{:S(2)}) copy-start(bf16[1,729,1152]{2,1,0:T(8,128)(2,1)} %add_convert_fusion.4) | copy-start | bytes 5038852
  373.2 150.3 %copy-start.34 = (bf16[4,729,16]{1,2,0:T(8,128)(2,1)}, bf16[4,729,16]{1,2,0:T(8,128)(2,1)S(1)}, u32[]{:S(2)}) copy-start(bf16[4,729,16]{1,2,0:T(8,128)(2,1)S(1)} %all-gather.1) | copy-start | bytes 279940
  579.8 238.6 %reduce-scatter.7.cloned.1.call-start = ((), (), s32[]{:S(2)}) async-start(), calls=%async_computation.11 | async-start | bytes 8478720 | tf_op jit(solution)/shard_map/reduce_scatter | solution.py:217
  605.9 245.4 %all-gather.25.cloned.1.call-start = ((), (), s32[]{:S(2)}) async-start(), calls=%async_computation.14 | async-start | bytes 5087232 | tf_op jit(solution)/shard_map/all_gather | solution.py:261
  696.8 121.6 %copy-start.18 = (bf16[1,729,1152]{2,1,0:T(8,128)(2,1)S(1)}, bf16[1,729,1152]{2,1,0:T(8,128)(2,1)}, u32[]{:S(2)}) copy-start(bf16[1,729,1152]{2,1,0:T(8,128)(2,1)} %reduce-scatter.9.cloned.1.call-done) | copy-start | bytes 5038852
  824.8 175.7 %all-reduce.11.cloned.1.call-start = ((), (), s32[]{:S(2)}) async-start(), calls=%async_computation.18 | async-start | bytes 1179648 | tf_op jit(solution)/shard_map/psum | solution.py:325
  824.9 8.8 copy-start.35
  833.7 13.3 %slice-start = ((s8[6782976]{0:T(1024)(128)(4,1)}), s8[2588672]{0:T(1024)(128)(4,1)S(1)}, s32[]{:S(2)}) async-start(s8[6782976]{0:T(1024)(128)(4,1)} %bitcast.261), calls=%async_computation.19 | async-start | bytes 5177344
  851.2 236.6 %all-reduce.9.cloned.1.call-start = ((), (), s32[]{:S(2)}) async-start(), calls=%async_computation.17 | async-start | bytes 2621440 | tf_op jit(solution)/shard_map/psum | solution.py:321
  863.4 99.9 %copy-start.26 = (f32[3,2,729,16]{2,3,0,1:T(8,128)S(1)}, f32[3,2,729,16]{2,3,0,1:T(8,128)}, u32[]{:S(2)}) copy-start(f32[3,2,729,16]{2,3,0,1:T(8,128)} %copy-done.25) | copy-start | bytes 839812
  863.8 10.1 copy-start.9
  863.9 10.1 copy-start.57
  873.9 8.1 copy-start.13
  882.1 12.7 %copy-start.58 = (bf16[2,729,8,72]{1,3,2,0:T(8,128)(2,1)}, bf16[2,729,8,72]{1,3,2,0:T(8,128)(2,1)S(1)}, u32[]{:S(2)}) copy-start(bf16[2,729,8,72]{1,3,2,0:T(8,128)(2,1)S(1)} %bitcast_dynamic-update-slice_fusion.11) | copy-start | bytes 5038852 | tf_op jit(solution)/shard_map/while
  894.8 13.3 %copy-start.6 = (bf16[2,729,8,72]{1,3,2,0:T(8,128)(2,1)S(1)}, bf16[2,729,8,72]{1,3,2,0:T(8,128)(2,1)}, u32[]{:S(2)}) copy-start(bf16[2,729,8,72]{1,3,2,0:T(8,128)(2,1)} %get-tuple-element.353) | copy-start | bytes 5038852 | tf_op jit(solution)/shard_map/while
  894.8 13.3 %copy-start.60 = (bf16[2,729,8,72]{1,3,2,0:T(8,128)(2,1)S(1)}, bf16[2,729,8,72]{1,3,2,0:T(8,128)(2,1)}, u32[]{:S(2)}) copy-start(bf16[2,729,8,72]{1,3,2,0:T(8,128)(2,1)} %get-tuple-element.340) | copy-start | bytes 5038852 | tf_op jit(solution)/shard_map/while
  913.8 10.1 copy-start.9
  913.8 10.1 copy-start.57
  923.8 8.1 copy-start.13
  931.9 12.6 copy-start.58
  944.5 13.1 %copy-start.6 = (bf16[2,729,8,72]{1,3,2,0:T(8,128)(2,1)S(1)}, bf16[2,729,8,72]{1,3,2,0:T(8,128)(2,1)}, u32[]{:S(2)}) copy-start(bf16[2,729,8,72]{1,3,2,0:T(8,128)(2,1)} %get-tuple-element.353) | copy-start | bytes 5038852 | tf_op jit(solution)/shard_map/while
  944.5 13.1 %copy-start.60 = (bf16[2,729,8,72]{1,3,2,0:T(8,128)(2,1)S(1)}, bf16[2,729,8,72]{1,3,2,0:T(8,128)(2,1)}, u32[]{:S(2)}) copy-start(bf16[2,729,8,72]{1,3,2,0:T(8,128)(2,1)} %get-tuple-element.340) | copy-start | bytes 5038852 | tf_op jit(solution)/shard_map/while
  963.3 9.1 copy-start.24
  972.4 262.2 %all-reduce.7.cloned.1.call-start = ((), (), s32[]{:S(2)}) async-start(), calls=%async_computation.16 | async-start | bytes 7077888 | tf_op jit(solution)/shard_map/psum | solution.py:317
  983.7 12.0 copy-start.12
  983.7 263.7 %reduce-scatter.11.cloned.1.call-start = ((), (), s32[]{:S(2)}) async-start(), calls=%async_computation.15 | async-start | bytes 5087232 | tf_op jit(solution)/shard_map/reduce_scatter | solution.py:292
  1234.6 12.7 %copy-start.40 = (f32[729]{0:T(1024)S(1)}, f32[729]{0:T(1024)}, u32[]{:S(2)}) copy-start(f32[729]{0:T(1024)} %copy-done.39) | copy-start | bytes 8752
  1234.6 12.7 %copy-start.43 = (f32[1152]{0:T(1024)S(1)}, f32[1152]{0:T(1024)}, u32[]{:S(2)}) copy-start(f32[1152]{0:T(1024)} %param.28) | copy-start | bytes 13828
  1234.7 12.7 %copy-start.48 = (f32[729]{0:T(1024)S(1)}, f32[729]{0:T(1024)}, u32[]{:S(2)}) copy-start(f32[729]{0:T(1024)} %copy-done.47) | copy-start | bytes 8752
  1251.1 9.0 copy-start.1
  (44 other events, 164.4 us)
Sparse Core Ops, SparseCore 0:
  18.0 15.1 all-gather.10
  35.0 55.7 all-gather.12
  92.7 30.1 all-gather.14
  178.5 11.2 reduce-scatter.4
  824.9 12.9 all-gather.24
  851.3 55.7 all-reduce.10
  972.6 115.1 all-reduce.8
  1094.9 139.7 all-reduce.6
  1237.0 10.2 reduce-scatter.10
Sparse Core Ops, SparseCore 1:
  181.9 123.2 all-gather.22
  306.9 37.9 all-gather.20
  346.6 39.7 all-gather.18
  387.9 123.2 all-gather.16
  579.9 116.8 reduce-scatter.8
  699.2 119.1 reduce-scatter.6
where the time goes:
time: 1270 us
  waiting for transfers between devices  781 us (61%)
  matrix products  326 us (26%)
  other arithmetic  77 us (6%)
  local copies, waits for them, and re-layouts  49.9 us (4%)
  between operations  18.4 us (1%)
  blocking collectives  13.3 us (1%)
    psum x1, waiting for transfers between devices, per_device(): lax.psum((grad_qkv_in_part, grad_proj_out_part, grad_up_in_part, grad_dow...  143 us
    all_gather x1, waiting for transfers between devices, per_device(): lax.all_gather(second_norm_reduced, 'tensor', axis=0, tiled=True)  125 us
    reduce_scatter x1, waiting for transfers between devices, per_device(): lax.psum_scatter(mlp_part.astype(jnp.bfloat16), 'tensor', scatter_dimensi...  118 us
    all_gather x1, waiting for transfers between devices, per_device(): grad_mlp_in = lax.all_gather(grad_mlp, 'tensor', axis=0, tiled=True)  103 us
    reduce_scatter x1, waiting for transfers between devices, per_device(): lax.psum_scatter(grad_ln2.astype(jnp.bfloat16), 'tensor', scatter_dimensi...  90.2 us
    psum x1, waiting for transfers between devices, per_device(): lax.psum((grad_qkv_out_part, grad_proj_in_part), ('fsdp', 'tensor'))  76.5 us
    all_gather x1, waiting for transfers between devices, per_device(): lax.all_gather(query_key_value_weight, 'fsdp', axis=0, tiled=True)  54.6 us
    unnamed x129, local copies, waits for them, and re-layouts  35.5 us
  transfers between devices with their start and end apart: 15, of which 12 were waited for; matrix products, arithmetic and copies ran while one was open for 27% of the time, Pallas kernels for 0%

commit v1 on v0

--- a/solution.py
+++ b/solution.py
@@ -6,6 +6,17 @@
 HEAD_DIM = 72
 highest_precision = lax.Precision.HIGHEST
 norm_eps = 1e-06
+
+
+def collect(shard, axis, dim):
+    ways = lax.axis_size(axis)
+    pieces = [shard]
+    for far in range(1, ways):
+        pieces.append(
+            lax.ppermute(pieces[far - 1], axis, [(d, (d - 1) % ways) for d in range(ways)])
+        )
+    line = jnp.concatenate(pieces, axis=dim)
+    return jnp.roll(line, lax.axis_index(axis) * shard.shape[dim], axis=dim)
 
 
 def normalize(values, gain, bias):
@@ -185,7 +196,7 @@
         preferred_element_type=jnp.float32,
     ).astype(jnp.bfloat16)
     ln2_in, up_mid_in = (
-        lax.all_gather(second_norm_reduced, "tensor", axis=0, tiled=True),
+        collect(second_norm_reduced, "tensor", 0),
         lax.all_gather(up_adapter_middle, "tensor", axis=0, tiled=True),
     )
     up_cols, down_cols, bias_cols = (up_rows, down_rows, up_projection_bias)

time: 1270 us -> 1230 us (0.969)
  waiting for transfers between devices: 781 us -> 685 us
  blocking collectives: 13.3 us -> 42.7 us
  local copies, waits for them, and re-layouts: 49.9 us -> 65 us
    all_gather x1 -> x0, waiting for transfers between devices: 125 us -> none  [per_device(): lax.all_gather(second_norm_reduced, 'tensor', axis=0, tiled=True)]
    all_gather x1, waiting for transfers between devices: 103 us -> 146 us  [per_device(): grad_mlp_in = lax.all_gather(grad_mlp, 'tensor', axis=0, tiled=True)]
    all_gather x1, waiting for transfers between devices: 34.9 us -> 0.01 us  [per_device(): lax.all_gather(down_weight, 'fsdp', axis=0, tiled=True)]
    ppermute x0 -> x3, waiting for transfers between devices: none -> 30.1 us  [collect(): lax.ppermute(pieces[far - 1], axis, [(d, (d - 1) % ways) for d in range(w...]
    all_gather x1, blocking collectives: 13.3 us -> 42.7 us  [per_device(): lax.all_gather(up_adapter_middle, 'tensor', axis=0, tiled=True)]
    all_gather x1, waiting for transfers between devices: 13.1 us -> 0.01 us  [per_device(): lax.all_gather(up_weight, 'fsdp', axis=0, tiled=True)]
    unnamed x129, local copies, waits for them, and re-layouts: 35.5 us -> 48.4 us
  transfers between devices with their start and end apart: 15 -> 17, of which waited for: 12 -> 10; matrix products, arithmetic and copies ran while one was open for 27% -> 29% of each run, Pallas kernels for 0% -> 0%
where the time goes in v1:
time: 1230 us
  waiting for transfers between devices  685 us (56%)
  matrix products  328 us (27%)
  other arithmetic  76.6 us (6%)
  local copies, waits for them, and re-layouts  65 us (5%)
  blocking collectives  42.7 us (3%)
  between operations  17 us (1%)
  starting transfers between devices  13.2 us (1%)
    all_gather x1, waiting for transfers between devices, per_device(): grad_mlp_in = lax.all_gather(grad_mlp, 'tensor', axis=0, tiled=True)  146 us
    psum x1, waiting for transfers between devices, per_device(): lax.psum((grad_qkv_in_part, grad_proj_out_part, grad_up_in_part, grad_dow...  143 us
    reduce_scatter x1, waiting for transfers between devices, per_device(): lax.psum_scatter(mlp_part.astype(jnp.bfloat16), 'tensor', scatter_dimensi...  118 us
    reduce_scatter x1, waiting for transfers between devices, per_device(): lax.psum_scatter(grad_ln2.astype(jnp.bfloat16), 'tensor', scatter_dimensi...  93.7 us
    psum x1, waiting for transfers between devices, per_device(): lax.psum((grad_qkv_out_part, grad_proj_in_part), ('fsdp', 'tensor'))  76.4 us
    all_gather x1, waiting for transfers between devices, per_device(): lax.all_gather(query_key_value_weight, 'fsdp', axis=0, tiled=True)  54.6 us
    unnamed x129, local copies, waits for them, and re-layouts  48.4 us
    all_gather x1, blocking collectives, per_device(): lax.all_gather(up_adapter_middle, 'tensor', axis=0, tiled=True)  42.7 us
  transfers between devices with their start and end apart: 17, of which 10 were waited for; matrix products, arithmetic and copies ran while one was open for 29% of the time, Pallas kernels for 0%

profile of v1, /device:TPU:0, one launch (start us, length us, event | category | flops | bytes accessed | tf_op | source)
XLA Modules:
  0.0 1228.6 jit_solution(9868067713363396942)
XLA Ops:
  7.3 4.7 reduce_sum.90
  25.0 7.4 all-gather.10.cloned.1.call-done
  35.4 54.6 %all-gather.12.cloned.1.call-done = bf16[1152,3,576]{2,0,1:T(8,128)(2,1)} async-done(((bf16[288,3,576]{2,0,1:T(8,128)(2,1)}), bf16[1152,3,576]{2,0,1:T(8,128)(2,1)}) %all-gather.12.cloned.1.call-update) | async-done | bytes 3981328 | tf_op jit(solution)/shard_map/all_gather | solution.py:131
  90.0 10.7 fusion.62
  100.8 5.4 fusion.51
  108.3 57.2 %while.28 = (s32[]{:T(128)}, bf16[2,729,8,72]{1,3,2,0:T(8,128)(2,1)}, f32[2,8,729]{2,1,0:T(8,128)S(1)}, bf16[2,729,8,72]{1,3,2,0:T(8,128)(2,1)}, bf16[2,729,8,72...) while((s32[]{:T(128)}, bf16[2,729,8,72]{1,3,2,0:T(8,128)(2,1)}, ...), condition=%wide.region_5.6_spmd, body=%wide.region_2.5_spmd.sunk | while | flops 1263117824 | bytes 55831608 | solution.py:171
  108.3 9.9 multiply_reduce_fusion.8
  118.2 9.2 fusion.208
  127.4 9.3 fusion.209
  136.7 9.9 multiply_reduce_fusion.8
  146.5 9.2 fusion.208
  155.7 9.3 fusion.209
  168.0 5.0 fusion.86
  181.6 7.4 reduce-scatter.5.cloned.1.call-done
  204.7 30.1 %collective-permute-done = bf16[1,729,1152]{2,1,0:T(8,128)(2,1)} collective-permute-done((bf16[1,729,1152]{2,1,0:T(8,128)(2,1)S(1)}, bf16[1,729,1152]{2,1,0:T(8,128)(2,1)}, u32[]{:S(2)}, u32[]{:S(2)}) %collective-permute-start) | collective-permute-done | bytes 1679648 | tf_op jit(solution)/shard_map/ppermute | solution.py:16
  239.2 145.7 %all-gather.20.cloned.1.call-done = bf16[4,729,1152]{2,1,0:T(8,128)(2,1)} async-done(((bf16[1,729,1152]{2,1,0:T(8,128)(2,1)}), bf16[4,729,1152]{2,1,0:T(8,128)(2,1)}) %all-gather.20.cloned.1.call-update) | async-done | bytes 6718480 | tf_op jit(solution)/shard_map/all_gather | solution.py:233
  384.9 14.8 %fusion.72 = f32[4,729,1076]{1,2,0:T(8,128)} fusion(bf16[4,729,1152]{2,1,0:T(8,128)(2,1)} %all-gather.20.cloned.1.call-done, bf16[1152,1076]{1,0:T(8,128)(2,1)} %all-gather.18.cloned.1.call-done), kind=kOutput, calls=%fused_computation.117 | convolution fusion | flops 7229067264 | bytes 21748032 | tf_op jit(solution)/shard_map/isd,df->isf/dot_general | solution.py:237
  406.8 42.7 %all-gather.1 = bf16[4,729,16]{1,2,0:T(8,128)(2,1)S(1)} all-gather(bf16[1,729,16]{1,2,0:T(8,128)(2,1)S(1)} %fusion.94), channel_id=2, replica_groups=mesh['fsdp'=4,'heads'=2,'tensor'=4] {'tensor'}, dimensions={0}, use_global_device_ids=true | all-gather | bytes 116640 | tf_op jit(solution)/shard_map/all_gather | solution.py:200
  449.6 6.6 fusion.141
  471.4 21.2 %multiply_convert_fusion.1 = (bf16[4,729,1076]{1,2,0:T(8,128)(2,1)}, f32[4,729,1076]{1,2,0:T(8,128)}) fusion(f32[4,729,1076]{1,2,0:T(8,128)} %fusion.141, f32[1076]{0:T(1024)S(1)} %convert_element_type.104, bf16[1152,1076]{1,0:T(8,128)(2,1)} %all-gather.16.cloned.1.call-done, bf16[8,729,1152]{2,1,0:T(8,128)(2,1)} %constant_dynamic-update-slice_fusion, ...), kind=kOutput, calls=%fused_computation.73 | convolution fusion | flops 7263580160 | bytes 41538228 | tf_op jit(solution)/shard_map/isd,df->isf/dot_general | solution.py:208
  492.6 18.5 %fusion.50 = bf16[4,729,1076]{1,2,0:T(8,128)(2,1)S(1)} fusion(f32[4,729,1076]{1,2,0:T(8,128)} %get-tuple-element.206, f32[4,729,1076]{1,2,0:T(8,128)} %fusion.72, f32[4,16,729]{2,1,0:T(8,128)S(1)} %fusion.143, bf16[4,16,1076]{2,1,0:T(8,128)(2,1)S(1)} %gather_fusion.7), kind=kOutput, calls=%fused_computation.72 | convolution fusion | flops 668312192 | bytes 31700512 | tf_op jit(solution)/shard_map/cbd,cdp->cbp/dot_general | solution.py:238
  514.8 13.2 %fusion.76 = f32[4,729,1152]{2,1,0:T(8,128)} fusion(bf16[4,729,1076]{1,2,0:T(8,128)(2,1)S(1)} %fusion.50, bf16[1152,1076]{1,0:T(8,128)(2,1)S(1)} %copy-done.53), kind=kOutput, calls=%fused_computation.121 | convolution fusion | flops 7229067264 | bytes 22191264 | tf_op jit(solution)/shard_map/isf,df->isd/dot_general | solution.py:246
  528.0 10.8 add_convert_fusion
  542.9 12.9 %fusion.74 = f32[4,729,1152]{2,1,0:T(8,128)S(1)} fusion(bf16[4,729,1076]{1,2,0:T(8,128)(2,1)} %get-tuple-element.205, bf16[1152,1076]{1,0:T(8,128)(2,1)S(1)} %copy-done.52), kind=kOutput, calls=%fused_computation.119 | convolution fusion | flops 7229067264 | bytes 22191264 | tf_op jit(solution)/shard_map/isf,df->isd/dot_general | solution.py:221
  555.7 8.5 add_convert_fusion.1
  565.0 93.7 %reduce-scatter.9.cloned.1.call-done = bf16[1,729,1152]{2,1,0:T(8,128)(2,1)} async-done(((bf16[4,729,1152]{2,1,0:T(8,128)(2,1)}), bf16[1,729,1152]{2,1,0:T(8,128)(2,1)}) %reduce-scatter.9.cloned.1.call-update) | async-done | bytes 1679632 | tf_op jit(solution)/shard_map/reduce_scatter | solution.py:253
  662.4 118.0 %reduce-scatter.7.cloned.1.call-done = bf16[1,729,1152]{2,1,0:T(8,128)(2,1)} async-done(((bf16[4,729,1152]{2,1,0:T(8,128)(2,1)}), bf16[1,729,1152]{2,1,0:T(8,128)(2,1)}) %reduce-scatter.7.cloned.1.call-update) | async-done | bytes 1679632 | tf_op jit(solution)/shard_map/reduce_scatter | solution.py:228
  780.4 6.4 fusion.137
  786.9 7.5 fusion.149
  795.7 5.5 fusion.148
  802.5 5.1 fusion.53
  825.4 99.8 %while.29 = (s32[]{:T(128)}, bf16[2,729,8,72]{1,3,2,0:T(8,128)(2,1)}, bf16[2,729,8,72]{1,3,2,0:T(8,128)(2,1)}, bf16[2,729,8,72]{1,3,2,0:T(8,128)(2,1)}, bf16[2,7...) while((s32[]{:T(128)}, ...), condition=%wide.region_15.16_spmd, body=%wide.region_13.15_spmd.sunk | while | flops 3112952320 | bytes 200497152 | solution.py:283
  825.9 10.0 fusion.218
  835.9 8.1 bitcast_dynamic-update-slice_fusion.11
  844.1 12.7 %multiply_reduce_fusion.9 = (f32[8,729]{1,0:T(8,128)S(1)}, f32[8,729,729]{1,2,0:T(8,128)}) fusion(f32[8,729,729]{1,2,0:T(8,128)} %fusion.218, f32[8,729]{1,0:T(8,128)S(1)} %dynamic-slice_bitcast_fusion.2, bf16[2,729,8,72]{1,3,2,0:T(8,128)(2,1)S(1)} %copy-done.14, s32[]{:T(128)S(6)} %copy.194, bf16[2,729,8,72]{1,3,2,0:T(8,128)(2,1)S(1)} %copy-done.9), kind=kOutput, calls=%fused_computation.30.clone.1 | convolution fusion | flops 629220288 | bytes 35830624 | tf_op jit(solution)/shard_map/while/body/eval_jaxpr/qhd,khd->hqk/dot_general | solution.py:69
  856.8 13.2 %multiply_convert_fusion.3 = bf16[8,729,729]{1,2,0:T(8,128)(2,1)S(1)} fusion(f32[8,729,729]{1,2,0:T(8,128)} %get-tuple-element.307, f32[8,729,729]{1,2,0:T(8,128)} %fusion.218, f32[8,729]{1,0:T(8,128)S(1)} %get-tuple-element.308, f32[8,729]{1,0:T(8,128)S(1)} %dynamic-slice_bitcast_fusion.2), kind=kLoop, calls=%fused_computation.29.clone.1 | loop fusion | flops 21257640 | bytes 42561936 | tf_op jit(solution)/shard_map/while/body/eval_jaxpr/convert_element_type | solution.py:74
  875.7 10.0 fusion.218
  885.7 8.1 bitcast_dynamic-update-slice_fusion.11
  893.9 12.6 %multiply_reduce_fusion.9 = (f32[8,729]{1,0:T(8,128)S(1)}, f32[8,729,729]{1,2,0:T(8,128)}) fusion(f32[8,729,729]{1,2,0:T(8,128)} %fusion.218, f32[8,729]{1,0:T(8,128)S(1)} %dynamic-slice_bitcast_fusion.2, bf16[2,729,8,72]{1,3,2,0:T(8,128)(2,1)S(1)} %copy-done.14, s32[]{:T(128)S(6)} %copy.194, bf16[2,729,8,72]{1,3,2,0:T(8,128)(2,1)S(1)} %copy-done.9), kind=kOutput, calls=%fused_computation.30.clone.1 | convolution fusion | flops 629220288 | bytes 35830624 | tf_op jit(solution)/shard_map/while/body/eval_jaxpr/qhd,khd->hqk/dot_general | solution.py:69
  906.5 13.1 %multiply_convert_fusion.3 = bf16[8,729,729]{1,2,0:T(8,128)(2,1)S(1)} fusion(f32[8,729,729]{1,2,0:T(8,128)} %get-tuple-element.307, f32[8,729,729]{1,2,0:T(8,128)} %fusion.218, f32[8,729]{1,0:T(8,128)S(1)} %get-tuple-element.308, f32[8,729]{1,0:T(8,128)S(1)} %dynamic-slice_bitcast_fusion.2), kind=kLoop, calls=%fused_computation.29.clone.1 | loop fusion | flops 21257640 | bytes 42561936 | tf_op jit(solution)/shard_map/while/body/eval_jaxpr/convert_element_type | solution.py:74
  925.3 6.3 fusion.56
  945.6 11.9 fusion.60
  957.5 4.9 fusion.52
  966.1 7.2 copy.104
  973.2 76.4 %all-reduce.9.cloned.1.call-done = (f32[3,8,16,576]{3,1,2,0:T(8,128)}, f32[8,576,16]{1,0,2:T(8,128)}) async-done(((f32[3,8,16,576]{3,1,2,0:T(8,128)}, f32[8,576,16]{1,0,2:T(8,128)}), (f32[3,8,16,576]{3,1,2,0:T(8,128)}, f32[8,576,16]{1,0,2:T(8,128)})) %all-reduce.9.cloned.1.call-update) | async-done | bytes 1179664 | tf_op jit(solution)/shard_map/psum | solution.py:332
  1053.8 142.8 %all-reduce.7.cloned.1.call-done = (f32[3,8,1152,16]{2,1,3,0:T(8,128)}, f32[8,16,1152]{2,0,1:T(8,128)}, f32[8,1152,16]{1,0,2:T(8,128)}, f32[8,16,1152]{2,0,1:T(8,128)}) async-done(((f32[3,8,1152,16]{2,1,3,0:T(8,128)}, f32[8,16,1152]{2,0,1:T(8,128)}, f32[8,1152,16]{1,0,2:T(8,128)}, f32[8,16,1152]{2,0,1:T(8,128)}), (f32[3,8,1152,16]{2,1,3,0:T(8,128)}, f32[8,16,1152]{2,0,1:T(8,128)}, f32[8,1152,16]{1,0,2:T(8,128)}, ...) | async-done | bytes 3538960 | tf_op jit(solution)/shard_map/psum | solution.py:328
  1202.5 6.7 reduce-scatter.11.cloned.1.call-done
  1216.7 5.2 copy.105
  (276 shorter events, 148.3 us)
Async XLA Ops:
  7.2 17.2 %copy-start = (bf16[3,8,1152,16]{2,3,1,0:T(8,128)(2,1)S(1)}, bf16[3,8,1152,16]{2,3,1,0:T(8,128)(2,1)}, u32[]{:S(2)}) copy-start(bf16[3,8,1152,16]{2,3,1,0:T(8,128)(2,1)} %param.38) | copy-start | bytes 2654212
  7.2 25.2 %all-gather.10.cloned.1.call-start = ((), (), s32[]{:S(2)}) async-start(), calls=%async_computation.4 | async-start | bytes 5087232 | tf_op jit(solution)/shard_map/all_gather | solution.py:137
  17.0 73.0 %all-gather.12.cloned.1.call-start = ((), (), s32[]{:S(2)}) async-start(), calls=%async_computation.5 | async-start | bytes 5529600 | tf_op jit(solution)/shard_map/all_gather | solution.py:131
  17.8 150.2 %all-gather.14.cloned.1.call-start = ((), (), s32[]{:S(2)}) async-start(), calls=%async_computation.6 | async-start | bytes 1843200 | tf_op jit(solution)/shard_map/all_gather | solution.py:132
  18.5 170.4 %reduce-scatter.5.cloned.1.call-start = ((), (), s32[]{:S(2)}) async-start(), calls=%async_computation.7 | async-start | bytes 5087232 | tf_op jit(solution)/shard_map/reduce_scatter | solution.py:187
  24.4 76.4 %copy-start.32 = (bf16[2,3,16,576]{3,2,1,0:T(8,128)(2,1)}, bf16[2,3,16,576]{3,2,1,0:T(8,128)(2,1)S(1)}, u32[]{:S(2)}) copy-start(bf16[2,3,16,576]{3,2,1,0:T(8,128)(2,1)S(1)} %gather_fusion.2) | copy-start | bytes 331780
  25.0 75.8 %copy-start.12 = (bf16[2,3,1152,16]{2,3,1,0:T(8,128)(2,1)}, bf16[2,3,1152,16]{2,3,1,0:T(8,128)(2,1)S(1)}, u32[]{:S(2)}) copy-start(bf16[2,3,1152,16]{2,3,1,0:T(8,128)(2,1)S(1)} %gather_fusion.1) | copy-start | bytes 663556
  35.4 65.4 %copy-start.25 = (f32[3,2,729,16]{2,3,0,1:T(8,128)}, f32[3,2,729,16]{2,3,0,1:T(8,128)S(1)}, u32[]{:S(2)}) copy-start(f32[3,2,729,16]{2,3,0,1:T(8,128)S(1)} %fusion.88) | copy-start | bytes 839812
  108.3 57.2 %copy-start.21 = (bf16[2,576,16]{1,2,0:T(8,128)(2,1)S(1)}, bf16[2,576,16]{1,2,0:T(8,128)(2,1)}, u32[]{:S(2)}) copy-start(bf16[2,576,16]{1,2,0:T(8,128)(2,1)} %gather_fusion.3) | copy-start | bytes 110596
  177.5 61.7 %all-gather.18.cloned.1.call-start = ((), (), s32[]{:S(2)}) async-start(), calls=%async_computation.9 | async-start | bytes 3317760 | tf_op jit(solution)/shard_map/all_gather | solution.py:134
  178.1 206.8 %all-gather.20.cloned.1.call-start = ((), (), s32[]{:S(2)}) async-start(), calls=%async_computation.11 | async-start | bytes 8478720 | tf_op jit(solution)/shard_map/all_gather | solution.py:233
  181.5 289.8 %all-gather.16.cloned.1.call-start = ((), (), s32[]{:S(2)}) async-start(), calls=%async_computation.8 | async-start | bytes 3317760 | tf_op jit(solution)/shard_map/all_gather | solution.py:133
  192.6 8.1 copy-start.50
  192.6 8.2 copy-start.42
  192.6 8.7 copy-start.43
  192.6 10.9 copy-start.20
  194.5 40.3 %collective-permute-start = (bf16[1,729,1152]{2,1,0:T(8,128)(2,1)S(1)}, bf16[1,729,1152]{2,1,0:T(8,128)(2,1)}, u32[]{:S(2)}, u32[]{:S(2)}) collective-permute-start(bf16[1,729,1152]{2,1,0:T(8,128)(2,1)S(1)} %get-tuple-element.194), channel_id=1, source_target_pairs={{0,3},{1,0},{2,1},{3,2},{4,7},{5,4},{6,5},{7,6},{8,11},{9,8},{10,9... | collective-permute-start | bytes 5038856 | tf_op jit(solution)/shard_map/ppermute | solution.py:16
  198.1 460.6 %reduce-scatter.9.cloned.1.call-start = ((), (), s32[]{:S(2)}) async-start(), calls=%async_computation.12 | async-start | bytes 8478720 | tf_op jit(solution)/shard_map/reduce_scatter | solution.py:253
  234.8 164.9 %collective-permute-start.1 = (bf16[1,729,1152]{2,1,0:T(8,128)(2,1)}, bf16[1,729,1152]{2,1,0:T(8,128)(2,1)}, u32[]{:S(2)}, u32[]{:S(2)}) collective-permute-start(bf16[1,729,1152]{2,1,0:T(8,128)(2,1)} %collective-permute-done), channel_id=1, source_target_pairs={{0,3},{1,0},{2,1},{3,2},{4,7},{5,4},{6,5},{7,6},{8,11},{9,8},{10,9... | collective-permute-start | bytes 5038856 | tf_op jit(solution)/shard_map/ppermute | solution.py:16
  384.9 19.4 %copy-start.10 = (bf16[4,729,1152]{2,1,0:T(8,128)(2,1)S(1)}, bf16[4,729,1152]{2,1,0:T(8,128)(2,1)}, u32[]{:S(2)}) copy-start(bf16[4,729,1152]{2,1,0:T(8,128)(2,1)} %all-gather.20.cloned.1.call-done) | copy-start | bytes 20155396
  399.7 62.0 %collective-permute-start.2 = (bf16[1,729,1152]{2,1,0:T(8,128)(2,1)}, bf16[1,729,1152]{2,1,0:T(8,128)(2,1)S(1)}, u32[]{:S(2)}, u32[]{:S(2)}) collective-permute-start(bf16[1,729,1152]{2,1,0:T(8,128)(2,1)} %collective-permute-done.1), channel_id=1, source_target_pairs={{0,3},{1,0},{2,1},{3,2},{4,7},{5,4},{6,5},{7,6},{8,11},{9,8},{10,9... | collective-permute-start | bytes 5038856 | tf_op jit(solution)/shard_map/ppermute | solution.py:16
  538.8 241.6 %reduce-scatter.7.cloned.1.call-start = ((), (), s32[]{:S(2)}) async-start(), calls=%async_computation.10 | async-start | bytes 8478720 | tf_op jit(solution)/shard_map/reduce_scatter | solution.py:228
  564.3 249.0 %all-gather.22.cloned.1.call-start = ((), (), s32[]{:S(2)}) async-start(), calls=%async_computation.13 | async-start | bytes 5087232 | tf_op jit(solution)/shard_map/all_gather | solution.py:272
  658.7 121.7 %copy-start.18 = (bf16[1,729,1152]{2,1,0:T(8,128)(2,1)S(1)}, bf16[1,729,1152]{2,1,0:T(8,128)(2,1)}, u32[]{:S(2)}) copy-start(bf16[1,729,1152]{2,1,0:T(8,128)(2,1)} %reduce-scatter.9.cloned.1.call-done) | copy-start | bytes 5038852
  786.8 175.6 %all-reduce.11.cloned.1.call-start = ((), (), s32[]{:S(2)}) async-start(), calls=%async_computation.17 | async-start | bytes 1179648 | tf_op jit(solution)/shard_map/psum | solution.py:336
  795.7 13.3 %slice-start = ((s8[6782976]{0:T(1024)(128)(4,1)}), s8[2588672]{0:T(1024)(128)(4,1)S(1)}, s32[]{:S(2)}) async-start(s8[6782976]{0:T(1024)(128)(4,1)} %bitcast.257), calls=%async_computation.18 | async-start | bytes 5177344
  813.2 236.5 %all-reduce.9.cloned.1.call-start = ((), (), s32[]{:S(2)}) async-start(), calls=%async_computation.16 | async-start | bytes 2621440 | tf_op jit(solution)/shard_map/psum | solution.py:332
  825.4 99.8 %copy-start.26 = (f32[3,2,729,16]{2,3,0,1:T(8,128)S(1)}, f32[3,2,729,16]{2,3,0,1:T(8,128)}, u32[]{:S(2)}) copy-start(f32[3,2,729,16]{2,3,0,1:T(8,128)} %copy-done.25) | copy-start | bytes 839812
  825.9 10.0 copy-start.9
  825.9 10.0 copy-start.54
  835.9 8.1 copy-start.14
  844.1 12.7 %copy-start.55 = (bf16[2,729,8,72]{1,3,2,0:T(8,128)(2,1)}, bf16[2,729,8,72]{1,3,2,0:T(8,128)(2,1)S(1)}, u32[]{:S(2)}) copy-start(bf16[2,729,8,72]{1,3,2,0:T(8,128)(2,1)S(1)} %bitcast_dynamic-update-slice_fusion.11) | copy-start | bytes 5038852 | tf_op jit(solution)/shard_map/while
  856.8 13.3 %copy-start.6 = (bf16[2,729,8,72]{1,3,2,0:T(8,128)(2,1)S(1)}, bf16[2,729,8,72]{1,3,2,0:T(8,128)(2,1)}, u32[]{:S(2)}) copy-start(bf16[2,729,8,72]{1,3,2,0:T(8,128)(2,1)} %get-tuple-element.355) | copy-start | bytes 5038852 | tf_op jit(solution)/shard_map/while
  856.8 13.3 %copy-start.57 = (bf16[2,729,8,72]{1,3,2,0:T(8,128)(2,1)S(1)}, bf16[2,729,8,72]{1,3,2,0:T(8,128)(2,1)}, u32[]{:S(2)}) copy-start(bf16[2,729,8,72]{1,3,2,0:T(8,128)(2,1)} %get-tuple-element.342) | copy-start | bytes 5038852 | tf_op jit(solution)/shard_map/while
  875.7 10.0 copy-start.9
  875.7 10.0 copy-start.54
  885.7 8.1 copy-start.14
  893.9 12.6 %copy-start.55 = (bf16[2,729,8,72]{1,3,2,0:T(8,128)(2,1)}, bf16[2,729,8,72]{1,3,2,0:T(8,128)(2,1)S(1)}, u32[]{:S(2)}) copy-start(bf16[2,729,8,72]{1,3,2,0:T(8,128)(2,1)S(1)} %bitcast_dynamic-update-slice_fusion.11) | copy-start | bytes 5038852 | tf_op jit(solution)/shard_map/while
  906.5 13.1 %copy-start.6 = (bf16[2,729,8,72]{1,3,2,0:T(8,128)(2,1)S(1)}, bf16[2,729,8,72]{1,3,2,0:T(8,128)(2,1)}, u32[]{:S(2)}) copy-start(bf16[2,729,8,72]{1,3,2,0:T(8,128)(2,1)} %get-tuple-element.355) | copy-start | bytes 5038852 | tf_op jit(solution)/shard_map/while
  906.5 13.1 %copy-start.57 = (bf16[2,729,8,72]{1,3,2,0:T(8,128)(2,1)S(1)}, bf16[2,729,8,72]{1,3,2,0:T(8,128)(2,1)}, u32[]{:S(2)}) copy-start(bf16[2,729,8,72]{1,3,2,0:T(8,128)(2,1)} %get-tuple-element.342) | copy-start | bytes 5038852 | tf_op jit(solution)/shard_map/while
  925.3 9.1 copy-start.24
  934.3 262.2 %all-reduce.7.cloned.1.call-start = ((), (), s32[]{:S(2)}) async-start(), calls=%async_computation.15 | async-start | bytes 7077888 | tf_op jit(solution)/shard_map/psum | solution.py:328
  945.6 12.0 copy-start.13
  945.6 263.5 %reduce-scatter.11.cloned.1.call-start = ((), (), s32[]{:S(2)}) async-start(), calls=%async_computation.14 | async-start | bytes 5087232 | tf_op jit(solution)/shard_map/reduce_scatter | solution.py:303
  1196.6 12.6 %copy-start.38 = (f32[729]{0:T(1024)S(1)}, f32[729]{0:T(1024)}, u32[]{:S(2)}) copy-start(f32[729]{0:T(1024)} %copy-done.37) | copy-start | bytes 8752
  1196.6 12.6 %copy-start.41 = (f32[1152]{0:T(1024)S(1)}, f32[1152]{0:T(1024)}, u32[]{:S(2)}) copy-start(f32[1152]{0:T(1024)} %param.28) | copy-start | bytes 13828
  1196.6 12.6 %copy-start.45 = (f32[729]{0:T(1024)S(1)}, f32[729]{0:T(1024)}, u32[]{:S(2)}) copy-start(f32[729]{0:T(1024)} %copy-done.44) | copy-start | bytes 8752
  1212.9 9.0 copy-start.1
  (43 other events, 171.9 us)
Sparse Core Ops, SparseCore 0:
  17.1 15.1 all-gather.9
  34.2 55.7 all-gather.11
  91.9 30.1 all-gather.13
  177.6 11.2 reduce-scatter.4
  190.6 41.0 all-gather.17
  233.2 151.7 all-gather.19
  386.8 41.8 all-gather.15
  538.9 119.7 reduce-scatter.8
  661.1 119.1 reduce-scatter.6
  786.9 13.0 all-gather.21
  813.3 55.7 all-reduce.10
  934.5 115.1 all-reduce.8
  1056.8 139.7 all-reduce.6
  1198.8 10.2 reduce-scatter.10
